TPU v7x, 32 devices: a whole 2x2x4 slice. The times are simulated.
32 devices in a mesh: freq: 4 (over y, core), tcol: 8 (over z, x).
Axes of the slice: x: 2, y: 2, z: 4, core: 2. Of those that a mesh axis runs over, the one named last changes fastest.
Arguments:
- data: bfloat16 [4, 2, 4096, 128], P('freq', None, 'tcol'), may hold values from -6 to 6
- left_factor: bfloat16 [4, 2, 4096, 256], P('freq', None, 'tcol'), may hold values from -0.25 to 0.25
- right_factor: bfloat16 [4, 2, 4096, 256], P('freq', None, 'tcol'), may hold values from -0.1875 to 0.1875
- ranks: int32 [4, 8, 8], P('freq'), may hold values from 1 to 32
- freq_index: int32 [4], P('freq'), may hold values from 0 to 229
Outputs:
- wavefield: float32 [4, 2, 4096, 128], P('freq', None, 'tcol')
- residual: float32 [4, 2, 4096, 128], P('freq', None, 'tcol')
Inputs may be any that keep to these rules, and one draw needn't show every extreme that they name: `ranks`: the rank of each tile; factor columns at or beyond it are not part of the kernel.
All inputs are finite; a program needn't handle non-finite values.
Results may differ from a plain program's by a relative error of at most 0.006.
Values may be sent and summed in bfloat16 or wider, within the bound.
No kernel may reach another device: no remote copies, remote signals or barrier semaphores. Data moves between devices by JAX's collectives and lax.ppermute only.
A program may use at most 64 MiB of HBM per device.

v0:
```python
import jax
import jax.numpy as jnp
from jax import lax
from jax.sharding import PartitionSpec as P

ITERS = 3


def conj_left(factor, field):
    first = jnp.einsum(
        "ftq,fts->fqs", factor[:, 0], field[:, 0], preferred_element_type=jnp.float32
    )
    second = jnp.einsum(
        "ftq,fts->fqs", factor[:, 1], field[:, 1], preferred_element_type=jnp.float32
    )
    third = jnp.einsum(
        "ftq,fts->fqs", factor[:, 0], field[:, 1], preferred_element_type=jnp.float32
    )
    fourth = jnp.einsum(
        "ftq,fts->fqs", factor[:, 1], field[:, 0], preferred_element_type=jnp.float32
    )
    return jnp.stack([first + second, third - fourth], 1)


def plain_right(factor, coeffs):
    first = jnp.einsum(
        "ftq,fqs->fts", factor[:, 0], coeffs[:, 0], preferred_element_type=jnp.float32
    )
    second = jnp.einsum(
        "ftq,fqs->fts", factor[:, 1], coeffs[:, 1], preferred_element_type=jnp.float32
    )
    third = jnp.einsum(
        "ftq,fqs->fts", factor[:, 0], coeffs[:, 1], preferred_element_type=jnp.float32
    )
    fourth = jnp.einsum(
        "ftq,fqs->fts", factor[:, 1], coeffs[:, 0], preferred_element_type=jnp.float32
    )
    return jnp.stack([first - second, third + fourth], 1)


def body(data, left_factor, right_factor, ranks, freq_index):
    ntile = lax.axis_size("tcol")
    here = lax.axis_index("tcol")
    rank_width = left_factor.shape[3] // ntile
    levels = jnp.arange(rank_width)[None, None, :]
    column_ranks = lax.dynamic_slice_in_dim(ranks, here, 1, 2)[:, :, 0]
    row_ranks = lax.dynamic_slice_in_dim(ranks, here, 1, 1)[:, 0, :]
    colmask = (levels < column_ranks[:, :, None]).astype(jnp.float32).reshape(ranks.shape[0], -1)
    rowmask = (levels < row_ranks[:, :, None]).astype(jnp.float32).reshape(ranks.shape[0], -1)
    damping = (0.1 + 0.9 * freq_index.astype(jnp.float32) / 229.0)[:, None, None, None]
    residual = data.astype(jnp.float32)
    wavefield = jnp.zeros_like(residual)
    direction = jnp.zeros_like(residual)
    image = jnp.zeros_like(residual)
    for step in range(ITERS):
        coeffs = conj_left(left_factor, residual.astype(jnp.bfloat16))
        coeffs = (coeffs * rowmask[:, None, :, None]).astype(jnp.bfloat16)
        arrived = lax.all_to_all(coeffs, "tcol", split_axis=2, concat_axis=2, tiled=True)
        gradient = plain_right(right_factor, arrived) - damping * wavefield
        forward_coeffs = conj_left(right_factor, gradient.astype(jnp.bfloat16))
        forward_coeffs = (forward_coeffs * colmask[:, None, :, None]).astype(jnp.bfloat16)
        forward_arrived = lax.all_to_all(
            forward_coeffs, "tcol", split_axis=2, concat_axis=2, tiled=True
        )
        moved = plain_right(left_factor, forward_arrived)
        partial_sums = jnp.stack(
            [
                jnp.sum(moved * moved + damping * gradient * gradient, axis=(0, 1, 2)),
                jnp.sum(moved * image + damping * gradient * direction, axis=(0, 1, 2)),
                jnp.sum(image * image + damping * direction * direction, axis=(0, 1, 2)),
                jnp.sum(moved * residual - damping * gradient * wavefield, axis=(0, 1, 2)),
                jnp.sum(image * residual - damping * direction * wavefield, axis=(0, 1, 2)),
            ]
        )
        totals = lax.psum(partial_sums, ("freq", "tcol"))
        a11, a12, a22, b1, b2 = (totals[0], totals[1], totals[2], totals[3], totals[4])
        if step == 0:
            alpha = b1 / (1.1 * a11)
            beta = jnp.zeros_like(alpha)
        else:
            first = 1.1 * a11
            second = 1.1 * a22
            determinant = first * second - a12 * a12
            alpha = (b1 * second - a12 * b2) / determinant
            beta = (first * b2 - a12 * b1) / determinant
        direction = alpha * gradient + beta * direction
        image = alpha * moved + beta * image
        wavefield = wavefield + direction
        residual = residual - image
    return (wavefield, residual)


def solution(mesh):
    in_specs = (
        P("freq", None, "tcol", None),
        P("freq", None, "tcol", None),
        P("freq", None, "tcol", None),
        P("freq", None, None),
        P("freq"),
    )
    out_specs = (P("freq", None, "tcol", None), P("freq", None, "tcol", None))
    return jax.shard_map(body, mesh=mesh, in_specs=in_specs, out_specs=out_specs, check_vma=False)
```

profile of v0, /device:TPU:0, one launch (start us, length us, event | category | flops | bytes accessed | tf_op | source)
XLA Modules:
  0.0 213.9 jit_solution(10456277240478988102)
XLA Ops:
  0.7 0.7 copy-done
  1.5 1.2 fusion.116
  2.8 1.2 fusion.118
  4.4 0.3 fusion.22
  4.7 0.3 fusion.23
  5.1 0.8 copy.35
  5.9 7.3 %all-to-all-start = ((bf16[1,2,256,128]{3,1,0,2:T(2,128)(2,1)}), bf16[1,2,256,128]{3,1,0,2:T(2,128)(2,1)S(1)}, u32[]{:S(2)}, u32[]{:S(2)}) async-start(bf16[1,2,256,128]{3,1,0,2:T(2,128)(2,1)} %copy.35), calls=%async_computation | async-start | bytes 262144 | tf_op jit(solution)/shard_map/all_to_all | solution.py:58
  13.8 6.7 %all-to-all-done = bf16[1,2,256,128]{3,1,0,2:T(2,128)(2,1)S(1)} async-done(((bf16[1,2,256,128]{3,1,0,2:T(2,128)(2,1)}), bf16[1,2,256,128]{3,1,0,2:T(2,128)(2,1)S(1)}, u32[]{:S(2)}, u32[]{:S(2)}) %all-to-all-start) | async-done | bytes 131104 | tf_op jit(solution)/shard_map/all_to_all | solution.py:58
  20.7 0.2 fusion.82
  20.9 0.2 fusion.80
  21.1 0.2 fusion.11
  21.4 0.2 fusion.10
  22.1 0.2 fusion.20
  22.5 0.8 copy.38
  23.3 3.4 %all-to-all-start.1 = ((bf16[1,2,256,128]{3,1,0,2:T(2,128)(2,1)}), bf16[1,2,256,128]{3,1,0,2:T(2,128)(2,1)S(1)}, u32[]{:S(2)}, u32[]{:S(2)}) async-start(bf16[1,2,256,128]{3,1,0,2:T(2,128)(2,1)} %copy.38), calls=%async_computation.1 | async-start | bytes 262144 | tf_op jit(solution)/shard_map/all_to_all | solution.py:62
  26.8 7.1 %all-to-all-done.1 = bf16[1,2,256,128]{3,1,0,2:T(2,128)(2,1)S(1)} async-done(((bf16[1,2,256,128]{3,1,0,2:T(2,128)(2,1)}), bf16[1,2,256,128]{3,1,0,2:T(2,128)(2,1)S(1)}, u32[]{:S(2)}, u32[]{:S(2)}) %all-to-all-start.1) | async-done | bytes 131104 | tf_op jit(solution)/shard_map/all_to_all | solution.py:62
  34.1 0.2 fusion.114
  34.3 0.2 fusion.112
  34.6 0.2 fusion.9
  34.8 0.2 fusion.8
  35.1 0.4 fusion.39
  35.5 38.5 %psum.21 = f32[5,128]{1,0:T(8,128)S(1)} all-reduce(f32[5,128]{1,0:T(8,128)S(1)} %stack.179), channel_id=1, replica_groups=mesh['freq'=4,'tcol'=8] {'freq','tcol'}, use_global_device_ids=true, to_apply=%region_4.0 | all-reduce | flops 640 | bytes 5120 | tf_op jit(solution)/shard_map/psum | solution.py:75
  74.2 0.3 fusion.108
  74.5 0.3 fusion.110
  74.7 0.3 fusion.18
  75.0 0.3 fusion.19
  75.5 11.7 %all_to_all.30 = bf16[1,2,256,128]{3,1,0,2:T(2,128)(2,1)S(1)} all-to-all(bf16[1,2,256,128]{3,1,0,2:T(2,128)(2,1)S(1)} %copy.46), channel_id=1, replica_groups=mesh['freq'=4,'tcol'=8] {'tcol'}, dimensions={2} | all-to-all | bytes 262144 | tf_op jit(solution)/shard_map/all_to_all | solution.py:58
  87.4 0.2 fusion.74
  87.6 0.2 fusion.72
  87.9 0.2 fusion.7
  88.1 0.2 fusion.6
  89.5 9.7 %all_to_all.31 = bf16[1,2,256,128]{3,1,0,2:T(2,128)(2,1)S(1)} all-to-all(bf16[1,2,256,128]{3,1,0,2:T(2,128)(2,1)S(1)} %copy.49), channel_id=1, replica_groups=mesh['freq'=4,'tcol'=8] {'tcol'}, dimensions={2} | all-to-all | bytes 262144 | tf_op jit(solution)/shard_map/all_to_all | solution.py:62
  99.4 0.2 fusion.106
  99.6 0.2 fusion.104
  99.9 0.2 fusion.5
  100.1 0.2 fusion.4
  100.4 0.3 add_reduce_fusion.1
  100.8 0.3 copy-done.6
  101.0 0.6 subtract_reduce_fusion
  101.7 38.3 %psum.22 = f32[5,128]{1,0:T(8,128)S(1)} all-reduce(f32[5,128]{1,0:T(8,128)S(1)} %stack.197), channel_id=1, replica_groups=mesh['freq'=4,'tcol'=8] {'freq','tcol'}, use_global_device_ids=true, to_apply=%region_10.0 | all-reduce | flops 640 | bytes 5120 | tf_op jit(solution)/shard_map/psum | solution.py:75
  139.9 2.1 fusion.186
  142.0 0.3 fusion.100
  142.3 0.3 fusion.102
  142.5 0.3 fusion.14
  142.8 0.3 fusion.15
  143.3 11.7 %all_to_all.32 = bf16[1,2,256,128]{3,1,0,2:T(2,128)(2,1)S(1)} all-to-all(bf16[1,2,256,128]{3,1,0,2:T(2,128)(2,1)S(1)} %copy.56), channel_id=1, replica_groups=mesh['freq'=4,'tcol'=8] {'tcol'}, dimensions={2} | all-to-all | bytes 262144 | tf_op jit(solution)/shard_map/all_to_all | solution.py:58
  155.2 0.2 fusion.66
  155.4 0.2 fusion.64
  155.7 0.2 fusion.3
  155.9 0.2 fusion.2
  156.2 1.1 fusion.185
  157.9 0.2 fusion.13
  158.2 9.7 %all_to_all.33 = bf16[1,2,256,128]{3,1,0,2:T(2,128)(2,1)S(1)} all-to-all(bf16[1,2,256,128]{3,1,0,2:T(2,128)(2,1)S(1)} %copy.59), channel_id=1, replica_groups=mesh['freq'=4,'tcol'=8] {'tcol'}, dimensions={2} | all-to-all | bytes 262144 | tf_op jit(solution)/shard_map/all_to_all | solution.py:62
  168.1 0.2 fusion.98
  168.4 0.2 fusion.96
  168.6 0.2 fusion.1
  168.9 0.2 fusion
  169.1 0.5 copy-done.4
  169.7 0.3 copy-done.3
  169.9 0.7 fusion.37
  170.7 38.3 %psum.23 = f32[5,128]{1,0:T(8,128)S(1)} all-reduce(f32[5,128]{1,0:T(8,128)S(1)} %stack.215), channel_id=1, replica_groups=mesh['freq'=4,'tcol'=8] {'freq','tcol'}, use_global_device_ids=true, to_apply=%region_16.0 | all-reduce | flops 640 | bytes 5120 | tf_op jit(solution)/shard_map/psum | solution.py:75
  209.0 2.0 add_subtract_fusion
  210.9 2.0 copy.63
  213.0 1.0 copy.62
  (59 shorter events, 5.1 us)
Async XLA Ops:
  0.6 0.7 copy-start
  0.6 2.1 copy-start.2
  2.8 1.6 copy-start.8
  5.1 15.6 %copy-start.1 = (bf16[1,2,512,256]{3,2,1,0:T(8,128)(2,1)S(1)}, bf16[1,2,512,256]{3,2,1,0:T(8,128)(2,1)}, u32[]{:S(2)}) copy-start(bf16[1,2,512,256]{3,2,1,0:T(8,128)(2,1)} %param.7) | copy-start | bytes 1572868
  5.9 14.6 %all-to-all-start = ((bf16[1,2,256,128]{3,1,0,2:T(2,128)(2,1)}), bf16[1,2,256,128]{3,1,0,2:T(2,128)(2,1)S(1)}, u32[]{:S(2)}, u32[]{:S(2)}) async-start(bf16[1,2,256,128]{3,1,0,2:T(2,128)(2,1)} %copy.35), calls=%async_computation | async-start | bytes 262144 | tf_op jit(solution)/shard_map/all_to_all | solution.py:58
  23.3 10.7 %all-to-all-start.1 = ((bf16[1,2,256,128]{3,1,0,2:T(2,128)(2,1)}), bf16[1,2,256,128]{3,1,0,2:T(2,128)(2,1)S(1)}, u32[]{:S(2)}, u32[]{:S(2)}) async-start(bf16[1,2,256,128]{3,1,0,2:T(2,128)(2,1)} %copy.38), calls=%async_computation.1 | async-start | bytes 262144 | tf_op jit(solution)/shard_map/all_to_all | solution.py:62
  100.1 0.7 copy-start.5
  100.3 0.7 copy-start.6
  168.6 1.0 copy-start.4
  168.9 1.1 copy-start.3
  169.1 1.5 copy-start.7
where the time goes:
time: 215 us; the launch traced here: 214 us
  blocking collectives  158 us (73%)
  waiting for transfers between devices  13.8 us (6%)
  matrix products  13 us (6%)
  starting transfers between devices  10.7 us (5%)
  local copies, waits for them, and re-layouts  8.86 us (4%)
  other arithmetic  7.88 us (4%)
    psum x3, blocking collectives, body(): totals = lax.psum(partial_sums, ('freq', 'tcol'))  115 us
    all_to_all x2, blocking collectives, body(): lax.all_to_all(coeffs, 'tcol', split_axis=2, concat_axis=2, tiled=True)  23.4 us
    all_to_all x2, blocking collectives, body(): lax.all_to_all(forward_coeffs, 'tcol', split_axis=2, concat_axis=2, tiled...  19.5 us
    all_to_all x1, starting transfers between devices, body(): lax.all_to_all(coeffs, 'tcol', split_axis=2, concat_axis=2, tiled=True)  7.28 us
    all_to_all x1, waiting for transfers between devices, body(): lax.all_to_all(forward_coeffs, 'tcol', split_axis=2, concat_axis=2, tiled...  7.12 us
    all_to_all x1, waiting for transfers between devices, body(): lax.all_to_all(coeffs, 'tcol', split_axis=2, concat_axis=2, tiled=True)  6.69 us
    unnamed x21, local copies, waits for them, and re-layouts  5.08 us
  transfers between devices with their start and end apart: 2, of which 2 were waited for; matrix products, arithmetic and copies ran while one was open for 0% of the time, Pallas kernels for 0%

commit v1 on v0

--- a/solution.py
+++ b/solution.py
@@ -59,9 +59,19 @@
         gradient = plain_right(right_factor, arrived) - damping * wavefield
         forward_coeffs = conj_left(right_factor, gradient.astype(jnp.bfloat16))
         forward_coeffs = (forward_coeffs * colmask[:, None, :, None]).astype(jnp.bfloat16)
-        forward_arrived = lax.all_to_all(
-            forward_coeffs, "tcol", split_axis=2, concat_axis=2, tiled=True
-        )
+        ways, here_2 = (lax.axis_size("tcol"), lax.axis_index("tcol"))
+        width = forward_coeffs.shape[2] // ways
+        lengths = list(forward_coeffs.shape)
+        lengths[2] = width
+        height = lengths[2]
+        lengths[2] = height * ways
+        full = jnp.zeros(lengths, forward_coeffs.dtype)
+        for mask in range(ways):
+            part = lax.dynamic_slice_in_dim(forward_coeffs, (here_2 ^ mask) * width, width, axis=2)
+            if mask:
+                part = lax.ppermute(part, "tcol", [(d, d ^ mask) for d in range(ways)])
+            full = lax.dynamic_update_slice_in_dim(full, part, (here_2 ^ mask) * height, axis=2)
+        forward_arrived = full
         moved = plain_right(left_factor, forward_arrived)
         partial_sums = jnp.stack(
             [

time: 215 us -> 236 us (1.098)
  starting transfers between devices: 10.7 us -> 40.9 us
  blocking collectives: 158 us -> 138 us
  local copies, waits for them, and re-layouts: 8.86 us -> 26.1 us
  waiting for transfers between devices: 13.8 us -> 6.72 us
    ppermute x0 -> x21, starting transfers between devices: none -> 33.6 us  [body(): part = lax.ppermute(part, 'tcol', [(d, d ^ mask) for d in range(ways)])]
    all_to_all x2 -> x0, blocking collectives: 19.5 us -> none  [body(): lax.all_to_all(forward_coeffs, 'tcol', split_axis=2, concat_axis=2, tiled...]
    dynamic_update_slice x0 -> x24, local copies, waits for them, and re-layouts: none -> 17.4 us  [body(): lax.dynamic_update_slice_in_dim(full, part, (here_2 ^ mask) * height, axi...]
    all_to_all x1 -> x0, waiting for transfers between devices: 7.12 us -> none  [body(): lax.all_to_all(forward_coeffs, 'tcol', split_axis=2, concat_axis=2, tiled...]
    all_to_all x1 -> x0, starting transfers between devices: 3.37 us -> none  [body(): lax.all_to_all(forward_coeffs, 'tcol', split_axis=2, concat_axis=2, tiled...]
    unnamed x21 -> x27, local copies, waits for them, and re-layouts: 5.08 us -> 5.71 us
  transfers between devices with their start and end apart: 2 -> 22, of which waited for: 2 -> 1; matrix products, arithmetic and copies ran while one was open for 0% -> 6% of each run, Pallas kernels for 0% -> 0%
where the time goes in v1:
time: 236 us; the launch traced here: 235 us
  blocking collectives  138 us (58%)
  starting transfers between devices  40.9 us (17%)
  local copies, waits for them, and re-layouts  26.1 us (11%)
  matrix products  12.9 us (5%)
  other arithmetic  7.89 us (3%)
  waiting for transfers between devices  6.72 us (3%)
    psum x3, blocking collectives, body(): totals = lax.psum(partial_sums, ('freq', 'tcol'))  113 us
    ppermute x21, starting transfers between devices, body(): part = lax.ppermute(part, 'tcol', [(d, d ^ mask) for d in range(ways)])  33.6 us
    all_to_all x2, blocking collectives, body(): lax.all_to_all(coeffs, 'tcol', split_axis=2, concat_axis=2, tiled=True)  25.5 us
    dynamic_update_slice x24, local copies, waits for them, and re-layouts, body(): lax.dynamic_update_slice_in_dim(full, part, (here_2 ^ mask) * height, axi...  17.4 us
    all_to_all x1, starting transfers between devices, body(): lax.all_to_all(coeffs, 'tcol', split_axis=2, concat_axis=2, tiled=True)  7.28 us
    all_to_all x1, waiting for transfers between devices, body(): lax.all_to_all(coeffs, 'tcol', split_axis=2, concat_axis=2, tiled=True)  6.67 us
    unnamed x27, local copies, waits for them, and re-layouts  5.71 us
  transfers between devices with their start and end apart: 22, of which 1 were waited for; matrix products, arithmetic and copies ran while one was open for 6% of the time, Pallas kernels for 0%

profile of v1, /device:TPU:0, one launch (start us, length us, event | category | flops | bytes accessed | tf_op | source)
XLA Modules:
  0.0 235.0 jit_solution(5324757415346695663)
XLA Ops:
  0.7 0.7 copy-done
  1.5 1.2 fusion.116
  2.8 1.2 fusion.118
  5.1 0.8 copy.32
  5.9 7.3 %all-to-all-start = ((bf16[1,2,256,128]{3,1,0,2:T(2,128)(2,1)}), bf16[1,2,256,128]{3,1,0,2:T(2,128)(2,1)S(1)}, u32[]{:S(2)}, u32[]{:S(2)}) async-start(bf16[1,2,256,128]{3,1,0,2:T(2,128)(2,1)} %copy.32), calls=%async_computation | async-start | bytes 262144 | tf_op jit(solution)/shard_map/all_to_all | solution.py:58
  13.8 6.7 %all-to-all-done = bf16[1,2,256,128]{3,1,0,2:T(2,128)(2,1)S(1)} async-done(((bf16[1,2,256,128]{3,1,0,2:T(2,128)(2,1)}), bf16[1,2,256,128]{3,1,0,2:T(2,128)(2,1)S(1)}, u32[]{:S(2)}, u32[]{:S(2)}) %all-to-all-start) | async-done | bytes 131104 | tf_op jit(solution)/shard_map/all_to_all | solution.py:58
  22.8 1.3 collective-permute-start
  24.1 1.3 collective-permute-start.4
  25.4 0.9 collective-permute-start.2
  26.3 2.5 %collective-permute-start.3 = (bf16[1,2,32,128]{2,3,1,0:T(8,128)(2,1)S(1)}, bf16[1,2,32,128]{2,3,1,0:T(8,128)(2,1)S(1)}, u32[]{:S(2)}, u32[]{:S(2)}) collective-permute-start(bf16[1,2,32,128]{2,3,1,0:T(8,128)(2,1)S(1)} %get-tuple-element.52), channel_id=1, source_target_pairs={{0,4},{1,5},{2,6},{3,7},{4,0},{5,1},{6,2},{7,3},{8,12},{9,13},{10,... | collective-permute-start | bytes 49160 | tf_op jit(solution)/shard_map/ppermute | solution.py:72
  28.9 1.4 collective-permute-start.5
  30.3 3.6 %collective-permute-start.6 = (bf16[1,2,32,128]{2,3,1,0:T(8,128)(2,1)S(1)}, bf16[1,2,32,128]{2,3,1,0:T(8,128)(2,1)S(1)}, u32[]{:S(2)}, u32[]{:S(2)}) collective-permute-start(bf16[1,2,32,128]{2,3,1,0:T(8,128)(2,1)S(1)} %get-tuple-element.49), channel_id=1, source_target_pairs={{0,7},{1,6},{2,5},{3,4},{4,3},{5,2},{6,1},{7,0},{8,15},{9,14},{10,... | collective-permute-start | bytes 49160 | tf_op jit(solution)/shard_map/ppermute | solution.py:72
  34.1 0.3 dynamic_update_slice.72
  34.4 0.7 dynamic_update_slice.73
  35.2 0.7 dynamic_update_slice.74
  35.9 0.7 dynamic_update_slice.75
  37.0 0.7 dynamic_update_slice.77
  37.6 0.7 dynamic_update_slice.78
  38.3 0.7 dynamic_update_slice.79
  39.9 0.4 fusion.39
  40.4 39.0 %psum.21 = f32[5,128]{1,0:T(8,128)S(1)} all-reduce(f32[5,128]{1,0:T(8,128)S(1)} %stack.179), channel_id=1, replica_groups=mesh['freq'=4,'tcol'=8] {'freq','tcol'}, use_global_device_ids=true, to_apply=%region_4.0 | all-reduce | flops 640 | bytes 5120 | tf_op jit(solution)/shard_map/psum | solution.py:85
  79.5 0.3 fusion.110
  80.9 12.4 %all_to_all.15 = bf16[1,2,256,128]{3,1,0,2:T(2,128)(2,1)S(1)} all-to-all(bf16[1,2,256,128]{3,1,0,2:T(2,128)(2,1)S(1)} %copy.40), channel_id=1, replica_groups=mesh['freq'=4,'tcol'=8] {'tcol'}, dimensions={2} | all-to-all | bytes 262144 | tf_op jit(solution)/shard_map/all_to_all | solution.py:58
  95.7 1.3 collective-permute-start.7
  97.0 1.3 collective-permute-start.11
  98.3 0.9 collective-permute-start.9
  99.2 2.5 %collective-permute-start.10 = (bf16[1,2,32,128]{2,3,1,0:T(8,128)(2,1)S(1)}, bf16[1,2,32,128]{2,3,1,0:T(8,128)(2,1)}, u32[]{:S(2)}, u32[]{:S(2)}) collective-permute-start(bf16[1,2,32,128]{2,3,1,0:T(8,128)(2,1)S(1)} %get-tuple-element.42), channel_id=1, source_target_pairs={{0,4},{1,5},{2,6},{3,7},{4,0},{5,1},{6,2},{7,3},{8,12},{9,13},{10,... | collective-permute-start | bytes 49160 | tf_op jit(solution)/shard_map/ppermute | solution.py:72
  101.8 0.6 copy-done.9
  102.4 1.4 collective-permute-start.12
  103.8 3.6 %collective-permute-start.13 = (bf16[1,2,32,128]{2,3,1,0:T(8,128)(2,1)S(1)}, bf16[1,2,32,128]{2,3,1,0:T(8,128)(2,1)}, u32[]{:S(2)}, u32[]{:S(2)}) collective-permute-start(bf16[1,2,32,128]{2,3,1,0:T(8,128)(2,1)S(1)} %get-tuple-element.39), channel_id=1, source_target_pairs={{0,7},{1,6},{2,5},{3,4},{4,3},{5,2},{6,1},{7,0},{8,15},{9,14},{10,... | collective-permute-start | bytes 49160 | tf_op jit(solution)/shard_map/ppermute | solution.py:72
  107.5 0.3 dynamic_update_slice.80
  107.8 1.5 dynamic_update_slice.81
  109.3 0.7 dynamic_update_slice.82
  110.1 1.5 dynamic_update_slice.83
  111.5 1.0 dynamic_update_slice.84
  112.6 0.7 dynamic_update_slice.85
  113.3 0.7 dynamic_update_slice.86
  114.0 1.4 dynamic_update_slice.87
  116.4 0.3 add_reduce_fusion.1
  117.1 0.6 subtract_reduce_fusion
  117.7 36.9 %psum.22 = f32[5,128]{1,0:T(8,128)S(1)} all-reduce(f32[5,128]{1,0:T(8,128)S(1)} %stack.197), channel_id=1, replica_groups=mesh['freq'=4,'tcol'=8] {'freq','tcol'}, use_global_device_ids=true, to_apply=%region_10.0 | all-reduce | flops 640 | bytes 5120 | tf_op jit(solution)/shard_map/psum | solution.py:85
  154.5 2.1 fusion.188
  158.0 13.1 %all_to_all.16 = bf16[1,2,256,128]{3,1,0,2:T(2,128)(2,1)S(1)} all-to-all(bf16[1,2,256,128]{3,1,0,2:T(2,128)(2,1)S(1)} %copy.47), channel_id=1, replica_groups=mesh['freq'=4,'tcol'=8] {'tcol'}, dimensions={2} | all-to-all | bytes 262144 | tf_op jit(solution)/shard_map/all_to_all | solution.py:58
  172.2 1.1 fusion.187
  174.4 1.3 collective-permute-start.14
  175.7 1.3 collective-permute-start.18
  177.0 0.9 collective-permute-start.16
  177.9 2.5 %collective-permute-start.17 = (bf16[1,2,32,128]{2,3,1,0:T(8,128)(2,1)S(1)}, bf16[1,2,32,128]{2,3,1,0:T(8,128)(2,1)S(1)}, u32[]{:S(2)}, u32[]{:S(2)}) collective-permute-start(bf16[1,2,32,128]{2,3,1,0:T(8,128)(2,1)S(1)} %get-tuple-element.32), channel_id=1, source_target_pairs={{0,4},{1,5},{2,6},{3,7},{4,0},{5,1},{6,2},{7,3},{8,12},{9,13},{10,... | collective-permute-start | bytes 49160 | tf_op jit(solution)/shard_map/ppermute | solution.py:72
  180.5 1.4 collective-permute-start.19
  181.9 3.6 %collective-permute-start.20 = (bf16[1,2,32,128]{2,3,1,0:T(8,128)(2,1)S(1)}, bf16[1,2,32,128]{2,3,1,0:T(8,128)(2,1)S(1)}, u32[]{:S(2)}, u32[]{:S(2)}) collective-permute-start(bf16[1,2,32,128]{2,3,1,0:T(8,128)(2,1)S(1)} %get-tuple-element.29), channel_id=1, source_target_pairs={{0,7},{1,6},{2,5},{3,4},{4,3},{5,2},{6,1},{7,0},{8,15},{9,14},{10,... | collective-permute-start | bytes 49160 | tf_op jit(solution)/shard_map/ppermute | solution.py:72
  185.6 0.3 dynamic_update_slice.88
  185.9 0.7 dynamic_update_slice.89
  186.6 0.7 dynamic_update_slice.90
  187.4 0.7 dynamic_update_slice.91
  188.4 0.7 dynamic_update_slice.93
  189.1 0.7 dynamic_update_slice.94
  189.8 0.7 dynamic_update_slice.95
  191.4 0.6 copy-done.4
  192.0 0.3 copy-done.3
  192.3 0.7 fusion.37
  193.0 37.0 %psum.23 = f32[5,128]{1,0:T(8,128)S(1)} all-reduce(f32[5,128]{1,0:T(8,128)S(1)} %stack.215), channel_id=1, replica_groups=mesh['freq'=4,'tcol'=8] {'freq','tcol'}, use_global_device_ids=true, to_apply=%region_16.0 | all-reduce | flops 640 | bytes 5120 | tf_op jit(solution)/shard_map/psum | solution.py:85
  230.0 2.0 add_subtract_fusion
  231.9 2.0 copy.51
  234.0 1.0 copy.50
  (127 shorter events, 14.4 us)
Async XLA Ops:
  0.6 0.7 copy-start
  0.6 2.1 copy-start.2
  2.8 1.6 copy-start.8
  5.1 15.6 %copy-start.1 = (bf16[1,2,512,256]{3,2,1,0:T(8,128)(2,1)S(1)}, bf16[1,2,512,256]{3,2,1,0:T(8,128)(2,1)}, u32[]{:S(2)}) copy-start(bf16[1,2,512,256]{3,2,1,0:T(8,128)(2,1)} %param.7) | copy-start | bytes 1572868
  5.9 14.6 %all-to-all-start = ((bf16[1,2,256,128]{3,1,0,2:T(2,128)(2,1)}), bf16[1,2,256,128]{3,1,0,2:T(2,128)(2,1)S(1)}, u32[]{:S(2)}, u32[]{:S(2)}) async-start(bf16[1,2,256,128]{3,1,0,2:T(2,128)(2,1)} %copy.32), calls=%async_computation | async-start | bytes 262144 | tf_op jit(solution)/shard_map/all_to_all | solution.py:58
  22.7 6.1 %collective-permute-start.1 = (bf16[1,2,32,128]{2,3,1,0:T(8,128)(2,1)S(1)}, bf16[1,2,32,128]{2,3,1,0:T(8,128)(2,1)S(1)}, u32[]{:S(2)}, u32[]{:S(2)}) collective-permute-start(bf16[1,2,32,128]{2,3,1,0:T(8,128)(2,1)S(1)} %get-tuple-element.54), channel_id=1, source_target_pairs={{0,2},{1,3},{2,0},{3,1},{4,6},{5,7},{6,4},{7,5},{8,10},{9,11},{10,... | collective-permute-start | bytes 49160 | tf_op jit(solution)/shard_map/ppermute | solution.py:72
  22.8 7.5 %collective-permute-start = (bf16[1,2,32,128]{2,3,1,0:T(8,128)(2,1)S(1)}, bf16[1,2,32,128]{2,3,1,0:T(8,128)(2,1)S(1)}, u32[]{:S(2)}, u32[]{:S(2)}) collective-permute-start(bf16[1,2,32,128]{2,3,1,0:T(8,128)(2,1)S(1)} %get-tuple-element.55), channel_id=1, source_target_pairs={{0,1},{1,0},{2,3},{3,2},{4,5},{5,4},{6,7},{7,6},{8,9},{9,8},{10,11... | collective-permute-start | bytes 49160 | tf_op jit(solution)/shard_map/ppermute | solution.py:72
  24.1 12.8 %collective-permute-start.4 = (bf16[1,2,32,128]{2,3,1,0:T(8,128)(2,1)S(1)}, bf16[1,2,32,128]{2,3,1,0:T(8,128)(2,1)S(1)}, u32[]{:S(2)}, u32[]{:S(2)}) collective-permute-start(bf16[1,2,32,128]{2,3,1,0:T(8,128)(2,1)S(1)} %get-tuple-element.51), channel_id=1, source_target_pairs={{0,5},{1,4},{2,7},{3,6},{4,1},{5,0},{6,3},{7,2},{8,13},{9,12},{10,... | collective-permute-start | bytes 49160 | tf_op jit(solution)/shard_map/ppermute | solution.py:72
  25.4 10.5 %collective-permute-start.2 = (bf16[1,2,32,128]{2,3,1,0:T(8,128)(2,1)S(1)}, bf16[1,2,32,128]{2,3,1,0:T(8,128)(2,1)S(1)}, u32[]{:S(2)}, u32[]{:S(2)}) collective-permute-start(bf16[1,2,32,128]{2,3,1,0:T(8,128)(2,1)S(1)} %get-tuple-element.53), channel_id=1, source_target_pairs={{0,3},{1,2},{2,1},{3,0},{4,7},{5,6},{6,5},{7,4},{8,11},{9,10},{10,... | collective-permute-start | bytes 49160 | tf_op jit(solution)/shard_map/ppermute | solution.py:72
  26.3 10.3 %collective-permute-start.3 = (bf16[1,2,32,128]{2,3,1,0:T(8,128)(2,1)S(1)}, bf16[1,2,32,128]{2,3,1,0:T(8,128)(2,1)S(1)}, u32[]{:S(2)}, u32[]{:S(2)}) collective-permute-start(bf16[1,2,32,128]{2,3,1,0:T(8,128)(2,1)S(1)} %get-tuple-element.52), channel_id=1, source_target_pairs={{0,4},{1,5},{2,6},{3,7},{4,0},{5,1},{6,2},{7,3},{8,12},{9,13},{10,... | collective-permute-start | bytes 49160 | tf_op jit(solution)/shard_map/ppermute | solution.py:72
  28.9 8.8 %collective-permute-start.5 = (bf16[1,2,32,128]{2,3,1,0:T(8,128)(2,1)S(1)}, bf16[1,2,32,128]{2,3,1,0:T(8,128)(2,1)S(1)}, u32[]{:S(2)}, u32[]{:S(2)}) collective-permute-start(bf16[1,2,32,128]{2,3,1,0:T(8,128)(2,1)S(1)} %get-tuple-element.50), channel_id=1, source_target_pairs={{0,6},{1,7},{2,4},{3,5},{4,2},{5,3},{6,0},{7,1},{8,14},{9,15},{10,... | collective-permute-start | bytes 49160 | tf_op jit(solution)/shard_map/ppermute | solution.py:72
  30.3 8.0 %collective-permute-start.6 = (bf16[1,2,32,128]{2,3,1,0:T(8,128)(2,1)S(1)}, bf16[1,2,32,128]{2,3,1,0:T(8,128)(2,1)S(1)}, u32[]{:S(2)}, u32[]{:S(2)}) collective-permute-start(bf16[1,2,32,128]{2,3,1,0:T(8,128)(2,1)S(1)} %get-tuple-element.49), channel_id=1, source_target_pairs={{0,7},{1,6},{2,5},{3,4},{4,3},{5,2},{6,1},{7,0},{8,15},{9,14},{10,... | collective-permute-start | bytes 49160 | tf_op jit(solution)/shard_map/ppermute | solution.py:72
  95.6 6.1 %collective-permute-start.8 = (bf16[1,2,32,128]{2,3,1,0:T(8,128)(2,1)S(1)}, bf16[1,2,32,128]{2,3,1,0:T(8,128)(2,1)S(1)}, u32[]{:S(2)}, u32[]{:S(2)}) collective-permute-start(bf16[1,2,32,128]{2,3,1,0:T(8,128)(2,1)S(1)} %get-tuple-element.44), channel_id=1, source_target_pairs={{0,2},{1,3},{2,0},{3,1},{4,6},{5,7},{6,4},{7,5},{8,10},{9,11},{10,... | collective-permute-start | bytes 49160 | tf_op jit(solution)/shard_map/ppermute | solution.py:72
  95.7 8.1 %collective-permute-start.7 = (bf16[1,2,32,128]{2,3,1,0:T(8,128)(2,1)S(1)}, bf16[1,2,32,128]{2,3,1,0:T(8,128)(2,1)S(1)}, u32[]{:S(2)}, u32[]{:S(2)}) collective-permute-start(bf16[1,2,32,128]{2,3,1,0:T(8,128)(2,1)S(1)} %get-tuple-element.45), channel_id=1, source_target_pairs={{0,1},{1,0},{2,3},{3,2},{4,5},{5,4},{6,7},{7,6},{8,9},{9,8},{10,11... | collective-permute-start | bytes 49160 | tf_op jit(solution)/shard_map/ppermute | solution.py:72
  97.0 15.6 %collective-permute-start.11 = (bf16[1,2,32,128]{2,3,1,0:T(8,128)(2,1)S(1)}, bf16[1,2,32,128]{2,3,1,0:T(8,128)(2,1)S(1)}, u32[]{:S(2)}, u32[]{:S(2)}) collective-permute-start(bf16[1,2,32,128]{2,3,1,0:T(8,128)(2,1)S(1)} %get-tuple-element.41), channel_id=1, source_target_pairs={{0,5},{1,4},{2,7},{3,6},{4,1},{5,0},{6,3},{7,2},{8,13},{9,12},{10,... | collective-permute-start | bytes 49160 | tf_op jit(solution)/shard_map/ppermute | solution.py:72
  98.3 11.8 %collective-permute-start.9 = (bf16[1,2,32,128]{2,3,1,0:T(8,128)(2,1)S(1)}, bf16[1,2,32,128]{2,3,1,0:T(8,128)(2,1)}, u32[]{:S(2)}, u32[]{:S(2)}) collective-permute-start(bf16[1,2,32,128]{2,3,1,0:T(8,128)(2,1)S(1)} %get-tuple-element.43), channel_id=1, source_target_pairs={{0,3},{1,2},{2,1},{3,0},{4,7},{5,6},{6,5},{7,4},{8,11},{9,10},{10,... | collective-permute-start | bytes 49160 | tf_op jit(solution)/shard_map/ppermute | solution.py:72
  99.2 12.3 %collective-permute-start.10 = (bf16[1,2,32,128]{2,3,1,0:T(8,128)(2,1)S(1)}, bf16[1,2,32,128]{2,3,1,0:T(8,128)(2,1)}, u32[]{:S(2)}, u32[]{:S(2)}) collective-permute-start(bf16[1,2,32,128]{2,3,1,0:T(8,128)(2,1)S(1)} %get-tuple-element.42), channel_id=1, source_target_pairs={{0,4},{1,5},{2,6},{3,7},{4,0},{5,1},{6,2},{7,3},{8,12},{9,13},{10,... | collective-permute-start | bytes 49160 | tf_op jit(solution)/shard_map/ppermute | solution.py:72
  101.8 0.6 copy-start.9
  102.4 10.9 %collective-permute-start.12 = (bf16[1,2,32,128]{2,3,1,0:T(8,128)(2,1)S(1)}, bf16[1,2,32,128]{2,3,1,0:T(8,128)(2,1)S(1)}, u32[]{:S(2)}, u32[]{:S(2)}) collective-permute-start(bf16[1,2,32,128]{2,3,1,0:T(8,128)(2,1)S(1)} %get-tuple-element.40), channel_id=1, source_target_pairs={{0,6},{1,7},{2,4},{3,5},{4,2},{5,3},{6,0},{7,1},{8,14},{9,15},{10,... | collective-permute-start | bytes 49160 | tf_op jit(solution)/shard_map/ppermute | solution.py:72
  103.8 3.6 %copy-start.11 = (bf16[1,2,32,128]{2,3,1,0:T(8,128)(2,1)}, bf16[1,2,32,128]{2,3,1,0:T(8,128)(2,1)S(1)}, u32[]{:S(2)}) copy-start(bf16[1,2,32,128]{2,3,1,0:T(8,128)(2,1)S(1)} %collective-permute-done.7) | copy-start | bytes 49156
  103.8 10.1 %collective-permute-start.13 = (bf16[1,2,32,128]{2,3,1,0:T(8,128)(2,1)S(1)}, bf16[1,2,32,128]{2,3,1,0:T(8,128)(2,1)}, u32[]{:S(2)}, u32[]{:S(2)}) collective-permute-start(bf16[1,2,32,128]{2,3,1,0:T(8,128)(2,1)S(1)} %get-tuple-element.39), channel_id=1, source_target_pairs={{0,7},{1,6},{2,5},{3,4},{4,3},{5,2},{6,1},{7,0},{8,15},{9,14},{10,... | collective-permute-start | bytes 49160 | tf_op jit(solution)/shard_map/ppermute | solution.py:72
  107.8 1.5 copy-start.10
  116.1 0.7 copy-start.5
  116.4 0.7 copy-start.6
  174.4 6.1 %collective-permute-start.15 = (bf16[1,2,32,128]{2,3,1,0:T(8,128)(2,1)S(1)}, bf16[1,2,32,128]{2,3,1,0:T(8,128)(2,1)S(1)}, u32[]{:S(2)}, u32[]{:S(2)}) collective-permute-start(bf16[1,2,32,128]{2,3,1,0:T(8,128)(2,1)S(1)} %get-tuple-element.34), channel_id=1, source_target_pairs={{0,2},{1,3},{2,0},{3,1},{4,6},{5,7},{6,4},{7,5},{8,10},{9,11},{10,... | collective-permute-start | bytes 49160 | tf_op jit(solution)/shard_map/ppermute | solution.py:72
  174.4 7.5 %collective-permute-start.14 = (bf16[1,2,32,128]{2,3,1,0:T(8,128)(2,1)S(1)}, bf16[1,2,32,128]{2,3,1,0:T(8,128)(2,1)S(1)}, u32[]{:S(2)}, u32[]{:S(2)}) collective-permute-start(bf16[1,2,32,128]{2,3,1,0:T(8,128)(2,1)S(1)} %get-tuple-element.35), channel_id=1, source_target_pairs={{0,1},{1,0},{2,3},{3,2},{4,5},{5,4},{6,7},{7,6},{8,9},{9,8},{10,11... | collective-permute-start | bytes 49160 | tf_op jit(solution)/shard_map/ppermute | solution.py:72
  175.7 12.7 %collective-permute-start.18 = (bf16[1,2,32,128]{2,3,1,0:T(8,128)(2,1)S(1)}, bf16[1,2,32,128]{2,3,1,0:T(8,128)(2,1)S(1)}, u32[]{:S(2)}, u32[]{:S(2)}) collective-permute-start(bf16[1,2,32,128]{2,3,1,0:T(8,128)(2,1)S(1)} %get-tuple-element.31), channel_id=1, source_target_pairs={{0,5},{1,4},{2,7},{3,6},{4,1},{5,0},{6,3},{7,2},{8,13},{9,12},{10,... | collective-permute-start | bytes 49160 | tf_op jit(solution)/shard_map/ppermute | solution.py:72
  177.0 10.4 %collective-permute-start.16 = (bf16[1,2,32,128]{2,3,1,0:T(8,128)(2,1)S(1)}, bf16[1,2,32,128]{2,3,1,0:T(8,128)(2,1)S(1)}, u32[]{:S(2)}, u32[]{:S(2)}) collective-permute-start(bf16[1,2,32,128]{2,3,1,0:T(8,128)(2,1)S(1)} %get-tuple-element.33), channel_id=1, source_target_pairs={{0,3},{1,2},{2,1},{3,0},{4,7},{5,6},{6,5},{7,4},{8,11},{9,10},{10,... | collective-permute-start | bytes 49160 | tf_op jit(solution)/shard_map/ppermute | solution.py:72
  177.9 10.2 %collective-permute-start.17 = (bf16[1,2,32,128]{2,3,1,0:T(8,128)(2,1)S(1)}, bf16[1,2,32,128]{2,3,1,0:T(8,128)(2,1)S(1)}, u32[]{:S(2)}, u32[]{:S(2)}) collective-permute-start(bf16[1,2,32,128]{2,3,1,0:T(8,128)(2,1)S(1)} %get-tuple-element.32), channel_id=1, source_target_pairs={{0,4},{1,5},{2,6},{3,7},{4,0},{5,1},{6,2},{7,3},{8,12},{9,13},{10,... | collective-permute-start | bytes 49160 | tf_op jit(solution)/shard_map/ppermute | solution.py:72
  180.5 8.6 %collective-permute-start.19 = (bf16[1,2,32,128]{2,3,1,0:T(8,128)(2,1)S(1)}, bf16[1,2,32,128]{2,3,1,0:T(8,128)(2,1)S(1)}, u32[]{:S(2)}, u32[]{:S(2)}) collective-permute-start(bf16[1,2,32,128]{2,3,1,0:T(8,128)(2,1)S(1)} %get-tuple-element.30), channel_id=1, source_target_pairs={{0,6},{1,7},{2,4},{3,5},{4,2},{5,3},{6,0},{7,1},{8,14},{9,15},{10,... | collective-permute-start | bytes 49160 | tf_op jit(solution)/shard_map/ppermute | solution.py:72
  181.9 7.9 %collective-permute-start.20 = (bf16[1,2,32,128]{2,3,1,0:T(8,128)(2,1)S(1)}, bf16[1,2,32,128]{2,3,1,0:T(8,128)(2,1)S(1)}, u32[]{:S(2)}, u32[]{:S(2)}) collective-permute-start(bf16[1,2,32,128]{2,3,1,0:T(8,128)(2,1)S(1)} %get-tuple-element.29), channel_id=1, source_target_pairs={{0,7},{1,6},{2,5},{3,4},{4,3},{5,2},{6,1},{7,0},{8,15},{9,14},{10,... | collective-permute-start | bytes 49160 | tf_op jit(solution)/shard_map/ppermute | solution.py:72
  190.9 1.0 copy-start.4
  191.2 1.1 copy-start.3
  191.4 1.5 copy-start.7
